TPU v7x, 256 devices: a whole 4x4x8 slice. The times are simulated.
256 devices in a mesh: ens: 2 (over x_lo), sx: 16 (over x_hi, y, core), sy: 8 (over z).
Axes of the slice: x: 4 (x_hi: 2, x_lo: 2; x = x_hi * 2 + x_lo), y: 4, z: 8, core: 2. Of those that a mesh axis runs over, the one named last changes fastest.
Arguments:
- snapshots: bfloat16 [4, 4, 128, 512, 512], P('ens', None, 'sx', 'sy'), may hold values from -6 to 6
- coefficients: bfloat16 [4, 256, 512], P('ens'), may hold values from -0.125 to 0.125
- modes: bfloat16 [4, 128, 512, 256], P(None, 'sx', 'sy'), may hold values from -12 to 12
Outputs:
- new_modes: bfloat16 [4, 128, 512, 256], P(None, 'sx', 'sy')
- gram: float32 [256, 256], replicated
- proj: float32 [4, 256, 512], P('ens')
All inputs are finite; a program needn't handle non-finite values.
Results may differ from a plain program's by a relative error of at most 0.005.
Values may be sent and summed in bfloat16 or wider, within the bound.
No kernel may reach another device: no remote copies, remote signals or barrier semaphores. Data moves between devices by JAX's collectives and lax.ppermute only.
A program may use at most 64 MiB of HBM per device.

v0:
```python
import math
import jax
import jax.numpy as jnp
from jax import lax
from jax.sharding import PartitionSpec as P

ETA = 0.25
LAM = 0.5
TAU = 0.4


def padded_2(array, sides, width):
    for axis, dim in sides:
        size, length = (lax.axis_size(axis), array.shape[dim])
        up = [(i, (i + 1) % size) for i in range(size - 1)]
        down = [(j, i) for i, j in up]
        last = lax.slice_in_dim(array, length - width, length, axis=dim)
        leading = lax.slice_in_dim(array, 0, width, axis=dim)
        before = lax.ppermute(last, axis, up)
        after = lax.ppermute(leading, axis, down)
        array = jnp.concatenate([before, array, after], axis=dim)
    return array


def bend(field):
    padded = padded_2(field, (("sx", 1), ("sy", 2)), 1).astype(jnp.float32)
    centre = padded[:, 1:-1, 1:-1]
    beside_all = (
        padded[:, 2:, 1:-1] + padded[:, :-2, 1:-1] + padded[:, 1:-1, 2:] + padded[:, 1:-1, :-2]
    )
    return 4.0 * centre - beside_all


def local(snapshots, coefficients, modes):
    members, levels, rows_x, rows_y, frames = snapshots.shape
    width = modes.shape[3]
    local_cells = levels * rows_x * rows_y
    total_cells = local_cells * lax.axis_size("sx") * lax.axis_size("sy")
    flat_modes = modes.reshape(local_cells, width)
    series = snapshots.reshape(members, local_cells, frames)
    bent = bend(modes).reshape(local_cells, width)
    partial_grad = jnp.zeros((local_cells, width), jnp.float32)
    for member in range(members):
        fitted = jnp.dot(flat_modes, coefficients[member], preferred_element_type=jnp.float32)
        misfit = (fitted - series[member].astype(jnp.float32)).astype(jnp.bfloat16)
        partial_grad = partial_grad + jnp.einsum(
            "ct,rt->cr", misfit, coefficients[member], preferred_element_type=jnp.float32
        )
    grad_full = lax.psum(partial_grad, "ens")
    moved = (flat_modes.astype(jnp.float32) - ETA * (grad_full + LAM * bent)).astype(jnp.bfloat16)
    moved_f = moved.astype(jnp.float32)
    squares = lax.psum(jnp.sum(moved_f * moved_f, axis=0), ("sx", "sy"))
    raw_gram = jnp.einsum("cr,cs->rs", moved, moved, preferred_element_type=jnp.float32)
    raw_proj = jnp.einsum("cr,mct->mrt", moved, series, preferred_element_type=jnp.float32)
    gram_sum, proj_sum = lax.psum((raw_gram, raw_proj), ("sx", "sy"))
    shrink = jnp.maximum(0.0, 1.0 - TAU / jnp.sqrt(squares / total_cells + 1e-06))
    new_modes = (
        (moved_f * shrink[None, :]).astype(jnp.bfloat16).reshape(levels, rows_x, rows_y, width)
    )
    gram = shrink[:, None] * gram_sum * shrink[None, :] / total_cells
    projected = shrink[None, :, None] * proj_sum / math.sqrt(total_cells)
    return (new_modes, gram, projected)


def solution(mesh):
    in_specs = (P("ens", None, "sx", "sy", None), P("ens", None, None), P(None, "sx", "sy", None))
    out_specs = (P(None, "sx", "sy", None), P(), P("ens", None, None))
    return jax.shard_map(local, mesh=mesh, in_specs=in_specs, out_specs=out_specs, check_vma=False)
```

profile of v0, /device:TPU:6, one launch (start us, length us, event | category | flops | bytes accessed | tf_op | source)
XLA Modules:
  0.0 1324.0 jit_solution(10424352402243552512)
XLA Ops:
  7.2 0.0 copy-start.1
  7.2 0.0 all-reduce.4.cloned.1.call-start
  7.2 4.1 fusion.20
  11.3 0.0 copy-done.1
  11.3 4.2 fusion.9
  15.5 4.3 convolution_add_fusion
  19.8 0.0 all-reduce.4.cloned.1.call-update
  19.9 0.0 all-reduce.6.cloned.1.call-start
  19.9 1.9 collective-permute-start
  21.9 7.3 collective-permute-start.1
  29.1 0.7 collective-permute-done
  29.9 0.1 constant_dynamic-update-slice_fusion.1
  30.0 1.7 collective-permute-done.1
  31.7 0.1 fusion.21
  31.7 1.3 collective-permute-start.3
  33.0 4.5 collective-permute-start.2
  37.6 0.0 collective-permute-done.3
  37.6 1.6 collective-permute-done.2
  39.2 0.5 maximum_convert_fusion
  39.8 0.7 fusion.5
  40.5 56.4 %all-reduce.4.cloned.1.call-done = f32[2048,256]{1,0:T(8,128)} async-done(((f32[2048,256]{1,0:T(8,128)}), f32[2048,256]{1,0:T(8,128)}) %all-reduce.4.cloned.1.call-update) | async-done | bytes 2097168 | tf_op jit(solution)/shard_map/psum | solution.py:49
  96.9 0.0 copy-start
  96.9 2.5 fusion.2
  99.4 1.2 fusion.23
  100.6 0.0 copy-done
  100.6 2.2 convolution_bitcast_fusion
  102.9 0.0 all-reduce.6.cloned.1.call-update
  102.9 329.3 %psum.29 = f32[256]{0:T(256)S(1)} all-reduce(f32[256]{0:T(256)S(1)} %get-tuple-element.5), channel_id=1, replica_groups=mesh['ens'=2,'sx'=16,'sy'=8] {'sx','sy'}, use_global_device_ids=true, to_apply=%region_2.0 | all-reduce | flops 256 | bytes 2048 | tf_op jit(solution)/shard_map/psum | solution.py:52
  432.2 1.2 fusion.3
  433.4 879.7 %all-reduce.6.cloned.1.call-done = (f32[256,256]{1,0:T(8,128)}, f32[2,256,512]{2,1,0:T(8,128)}) async-done(((f32[256,256]{1,0:T(8,128)}, f32[2,256,512]{2,1,0:T(8,128)}), (f32[256,256]{1,0:T(8,128)}, f32[2,256,512]{2,1,0:T(8,128)})) %all-reduce.6.cloned.1.call-update) | async-done | bytes 1310736 | tf_op jit(solution)/shard_map/psum | solution.py:55
  1313.1 1.8 multiply_multiply_fusion.1
  1314.8 2.3 multiply_multiply_fusion
  (4 shorter events, 0.0 us)
Async XLA Ops:
  7.2 4.1 copy-start.1
  7.2 89.8 %all-reduce.4.cloned.1.call-start = ((), (), s32[]{:S(2)}) async-start(), calls=%async_computation | async-start | bytes 4194304 | tf_op jit(solution)/shard_map/psum | solution.py:49
  19.9 1293.2 %all-reduce.6.cloned.1.call-start = ((), (), s32[]{:S(2)}) async-start(), calls=%async_computation.1 | async-start | bytes 2621440 | tf_op jit(solution)/shard_map/psum | solution.py:55
  19.9 9.9 collective-permute-start
  21.9 9.8 collective-permute-start.1
  31.7 5.9 collective-permute-start.3
  33.0 6.2 collective-permute-start.2
  96.9 3.7 copy-start
Sparse Core Ops, SparseCore 0:
  20.0 76.9 all-reduce.3
  103.0 1210.0 all-reduce.5
where the time goes:
time: 1320 us
  waiting for transfers between devices  940 us (71%)
  blocking collectives  329 us (25%)
  starting transfers between devices  15.1 us (1%)
  between operations  14.1 us (1%)
    psum x1, waiting for transfers between devices, local(): gram_sum, proj_sum = lax.psum((raw_gram, raw_proj), ('sx', 'sy'))  880 us
    psum x1, blocking collectives, local(): squares = lax.psum(jnp.sum(moved_f * moved_f, axis=0), ('sx', 'sy'))  329 us
    psum x1, waiting for transfers between devices, local(): grad_full = lax.psum(partial_grad, 'ens')  56.4 us
  transfers between devices with their start and end apart: 6, of which 5 were waited for; matrix products, arithmetic and copies ran while one was open for 0% of the time, Pallas kernels for 0%

commit v1 on v0

--- a/solution.py
+++ b/solution.py
@@ -7,6 +7,9 @@
 ETA = 0.25
 LAM = 0.5
 TAU = 0.4
+state_squares_on_mesh = lambda body, mesh_ax, device_axis: lax.psum(
+    lax.psum(body, mesh_ax), device_axis
+)
 
 
 def padded_2(array, sides, width):
@@ -52,7 +55,7 @@
     squares = lax.psum(jnp.sum(moved_f * moved_f, axis=0), ("sx", "sy"))
     raw_gram = jnp.einsum("cr,cs->rs", moved, moved, preferred_element_type=jnp.float32)
     raw_proj = jnp.einsum("cr,mct->mrt", moved, series, preferred_element_type=jnp.float32)
-    gram_sum, proj_sum = lax.psum((raw_gram, raw_proj), ("sx", "sy"))
+    gram_sum, proj_sum = state_squares_on_mesh((raw_gram, raw_proj), "sy", "sx")
     shrink = jnp.maximum(0.0, 1.0 - TAU / jnp.sqrt(squares / total_cells + 1e-06))
     new_modes = (
         (moved_f * shrink[None, :]).astype(jnp.bfloat16).reshape(levels, rows_x, rows_y, width)

time: 1320 us -> 519 us (0.39)
  waiting for transfers between devices: 940 us -> 139 us
    psum x1 -> x2, waiting for transfers between devices: 880 us -> 78.9 us  [the longest x1 78.9 us: lax.psum(body, mesh_ax)]
  transfers between devices with their start and end apart: 6 -> 7, of which waited for: 5 -> 5; matrix products, arithmetic and copies ran while one was open for 0% -> 1% of each run, Pallas kernels for 0% -> 0%
where the time goes in v1:
time: 519 us
  blocking collectives  325 us (63%)
  waiting for transfers between devices  139 us (27%)
  starting transfers between devices  15.1 us (3%)
  between operations  13.8 us (3%)
  matrix products  12 us (2%)
  other arithmetic  9.05 us (2%)
    psum x1, blocking collectives, local(): squares = lax.psum(jnp.sum(moved_f * moved_f, axis=0), ('sx', 'sy'))  325 us
    psum x1, waiting for transfers between devices, lax.psum(body, mesh_ax)  78.9 us
    psum x1, waiting for transfers between devices, local(): grad_full = lax.psum(partial_grad, 'ens')  56.4 us
  transfers between devices with their start and end apart: 7, of which 5 were waited for; matrix products, arithmetic and copies ran while one was open for 1% of the time, Pallas kernels for 0%

profile of v1, /device:TPU:6, one launch (start us, length us, event | category | flops | bytes accessed | tf_op | source)
XLA Modules:
  0.0 518.7 jit_solution(17409823254863314090)
XLA Ops:
  7.2 0.0 copy-start.1
  7.2 0.0 all-reduce.6.cloned.1.call-start
  7.2 4.0 fusion.20
  11.3 0.0 copy-done.1
  11.3 4.2 fusion.9
  15.5 4.3 convolution_add_fusion
  19.8 0.0 all-reduce.6.cloned.1.call-update
  19.8 0.0 all-reduce.10.cloned.1.call-start
  19.9 1.9 collective-permute-start
  21.8 7.3 %collective-permute-start.1 = (bf16[4,1,64,256]{3,2,1,0:T(8,128)(2,1)S(1)}, bf16[4,1,64,256]{3,2,1,0:T(8,128)(2,1)S(1)}, u32[]{:S(2)}, u32[]{:S(2)}) collective-permute-start(bf16[4,1,64,256]{3,2,1,0:T(8,128)(2,1)S(1)} %get-tuple-element.13), channel_id=1, source_target_pairs={{8,0},{16,8},{24,16},{32,24},{40,32},{48,40},{56,48},{64,56},{72,6... | collective-permute-start | bytes 393224 | tf_op jit(solution)/shard_map/ppermute | solution.py:23
  29.1 0.7 collective-permute-done
  29.8 0.1 constant_dynamic-update-slice_fusion.1
  29.9 1.7 collective-permute-done.1
  31.6 0.1 fusion.21
  31.7 1.3 collective-permute-start.3
  33.0 4.5 collective-permute-start.2
  37.6 0.0 collective-permute-done.3
  37.6 1.6 collective-permute-done.2
  39.2 0.5 maximum_convert_fusion
  39.7 0.7 fusion.5
  40.5 56.4 %all-reduce.6.cloned.1.call-done = f32[2048,256]{1,0:T(8,128)} async-done(((f32[2048,256]{1,0:T(8,128)}), f32[2048,256]{1,0:T(8,128)}) %all-reduce.6.cloned.1.call-update) | async-done | bytes 2097168 | tf_op jit(solution)/shard_map/psum | solution.py:52
  96.9 0.0 copy-start
  96.9 2.5 fusion.2
  99.4 1.2 fusion.23
  100.6 0.0 copy-done
  100.6 2.2 convolution_bitcast_fusion
  102.8 0.0 all-reduce.10.cloned.1.call-update
  102.9 0.0 all-reduce.8.cloned.1.call-start
  102.9 78.9 %all-reduce.10.cloned.1.call-done = (f32[256,256]{1,0:T(8,128)}, f32[2,256,512]{2,1,0:T(8,128)}) async-done(((f32[256,256]{1,0:T(8,128)}, f32[2,256,512]{2,1,0:T(8,128)}), (f32[256,256]{1,0:T(8,128)}, f32[2,256,512]{2,1,0:T(8,128)})) %all-reduce.10.cloned.1.call-update) | async-done | bytes 1310736 | tf_op jit(solution)/shard_map/psum | solution.py:11
  181.8 0.0 all-reduce.8.cloned.1.call-update
  181.9 325.0 %psum.43 = f32[256]{0:T(256)S(1)} all-reduce(f32[256]{0:T(256)S(1)} %get-tuple-element.7), channel_id=1, replica_groups=mesh['ens'=2,'sx'=16,'sy'=8] {'sx','sy'}, use_global_device_ids=true, to_apply=%region_2.0 | all-reduce | flops 256 | bytes 2048 | tf_op jit(solution)/shard_map/psum | solution.py:55
  506.9 1.2 fusion.3
  508.1 0.0 all-reduce.8.cloned.1.call-done
  508.1 1.8 multiply_multiply_fusion.1
  509.9 2.3 multiply_multiply_fusion
  (4 shorter events, 0.1 us)
Async XLA Ops:
  7.2 4.1 copy-start.1
  7.2 89.7 %all-reduce.6.cloned.1.call-start = ((), (), s32[]{:S(2)}) async-start(), calls=%async_computation | async-start | bytes 4194304 | tf_op jit(solution)/shard_map/psum | solution.py:52
  19.8 162.0 %all-reduce.10.cloned.1.call-start = ((), (), s32[]{:S(2)}) async-start(), calls=%async_computation.2 | async-start | bytes 2621440 | tf_op jit(solution)/shard_map/psum | solution.py:11
  19.9 9.9 %collective-permute-start = (bf16[4,1,64,256]{3,2,1,0:T(8,128)(2,1)S(1)}, bf16[4,1,64,256]{3,2,1,0:T(8,128)(2,1)S(1)}, u32[]{:S(2)}, u32[]{:S(2)}) collective-permute-start(bf16[4,1,64,256]{3,2,1,0:T(8,128)(2,1)S(1)} %get-tuple-element.14), channel_id=1, source_target_pairs={{0,8},{8,16},{16,24},{24,32},{32,40},{40,48},{48,56},{56,64},{64,7... | collective-permute-start | bytes 393224 | tf_op jit(solution)/shard_map/ppermute | solution.py:22
  21.8 9.8 %collective-permute-start.1 = (bf16[4,1,64,256]{3,2,1,0:T(8,128)(2,1)S(1)}, bf16[4,1,64,256]{3,2,1,0:T(8,128)(2,1)S(1)}, u32[]{:S(2)}, u32[]{:S(2)}) collective-permute-start(bf16[4,1,64,256]{3,2,1,0:T(8,128)(2,1)S(1)} %get-tuple-element.13), channel_id=1, source_target_pairs={{8,0},{16,8},{24,16},{32,24},{40,32},{48,40},{56,48},{64,56},{72,6... | collective-permute-start | bytes 393224 | tf_op jit(solution)/shard_map/ppermute | solution.py:23
  31.7 5.9 %collective-permute-start.3 = (bf16[4,10,1,256]{3,2,1,0:T(2,128)(2,1)S(1)}, bf16[4,10,1,256]{3,2,1,0:T(2,128)(2,1)S(1)}, u32[]{:S(2)}, u32[]{:S(2)}) collective-permute-start(bf16[4,10,1,256]{3,2,1,0:T(2,128)(2,1)S(1)} %get-tuple-element.12), channel_id=1, source_target_pairs={{1,0},{2,1},{3,2},{4,3},{5,4},{6,5},{7,6},{9,8},{10,9},{11,10},{12... | collective-permute-start | bytes 61448 | tf_op jit(solution)/shard_map/ppermute | solution.py:23
  33.0 6.2 %collective-permute-start.2 = (bf16[4,10,1,256]{3,2,1,0:T(2,128)(2,1)S(1)}, bf16[4,10,1,256]{3,2,1,0:T(2,128)(2,1)S(1)}, u32[]{:S(2)}, u32[]{:S(2)}) collective-permute-start(bf16[4,10,1,256]{3,2,1,0:T(2,128)(2,1)S(1)} %get-tuple-element.11), channel_id=1, source_target_pairs={{0,1},{1,2},{2,3},{3,4},{4,5},{5,6},{6,7},{8,9},{9,10},{10,11},{11... | collective-permute-start | bytes 61448 | tf_op jit(solution)/shard_map/ppermute | solution.py:22
  96.9 3.7 copy-start
  102.9 405.2 %all-reduce.8.cloned.1.call-start = ((), (), s32[]{:S(2)}) async-start(), calls=%async_computation.1 | async-start | bytes 2621440 | tf_op jit(solution)/shard_map/psum | solution.py:10
Sparse Core Ops, SparseCore 0:
  20.0 76.9 all-reduce.5
  103.0 78.8 all-reduce.9
  184.8 145.3 all-reduce.7
